TPU v7x, 32 devices: a whole 2x2x4 slice. The times are simulated.
32 devices in a mesh: grp: 16 (over z, x, core), patch: 2 (over y).
Axes of the slice: x: 2, y: 2, z: 4, core: 2. Of those that a mesh axis runs over, the one named last changes fastest.
Arguments:
- tokens: bfloat16 [12288, 1152], P(('grp', 'patch')), parts along dimension 0, may hold values from -6 to 6
- projection_weight: bfloat16 [1152, 3456], replicated, may hold values from -0.1875 to 0.1875
- shift_term: float32 [1152], replicated, may hold values from -3 to 3
- scale_term: float32 [1152], replicated, may hold values from -3 to 3
- query_gain: float32 [72], replicated, may hold values from 0.1 to 1.9
- key_gain: float32 [72], replicated, may hold values from 0.1 to 1.9
- stale_keys: bfloat16 [12288, 1152], P(('grp', 'patch')), parts along dimension 0, may hold values from -6 to 6
- stale_values: bfloat16 [12288, 1152], P(('grp', 'patch')), parts along dimension 0, may hold values from -6 to 6
- stale_output: bfloat16 [12288, 1152], P(('grp', 'patch')), parts along dimension 0, may hold values from -3 to 3
- refreshed: int32 [768], P('grp'), parts along dimension 0, may hold values from 0 to 1, as said below
Outputs:
- attended: bfloat16 [12288, 1152], P(('grp', 'patch')), parts along dimension 0
There are 16 independent parts, one for each index of `grp`. A program takes and returns all parts, laid end to end along the dimension named above; an argument that names none is the same for every part. Nothing has to cross between parts.
Inputs may be any that keep to these rules, and one draw needn't show every extreme that they name: Exactly 16 of the 48 entries are 1; in every prompt some device has all 16 of its tiles refreshed.
All inputs are finite; a program needn't handle non-finite values.
Results may differ from a plain program's by a relative error of at most 0.0045.
Values may be sent and summed in bfloat16 or wider, within the bound.
No kernel may reach another device: no remote copies, remote signals or barrier semaphores. Data moves between devices by JAX's collectives and lax.ppermute only.
A program may use at most 128 MiB of HBM per device.

v0:
```python
import math
import jax
import jax.numpy as jnp
from jax import lax
from jax.sharding import PartitionSpec as P

H = 16
TILE = 16
epsilon = 1e-06


def modulate(row_block, shift_term, scale_term):
    values = row_block.astype(jnp.float32)
    center = values - jnp.mean(values, axis=-1, keepdims=True)
    spread = jnp.mean(center * center, axis=-1, keepdims=True)
    normed = center / jnp.sqrt(spread + epsilon)
    return (normed * (1.0 + scale_term) + shift_term).astype(jnp.bfloat16)


def head_norm(row_block, gain_vector, head_count):
    values = row_block.astype(jnp.float32).reshape(row_block.shape[0], head_count, -1)
    normed = values / jnp.sqrt(jnp.mean(values * values, axis=-1, keepdims=True) + epsilon)
    return (normed * gain_vector).astype(jnp.bfloat16).reshape(row_block.shape[0], -1)


def block_size(row_total, row_unit):
    multiple = row_total // row_unit
    chosen = 1
    for candidate in range(1, multiple + 1):
        if multiple % candidate == 0 and candidate * row_unit <= 1024:
            chosen = candidate
    return chosen * row_unit


def partial_terms(queries, key_rows, values, head_count):
    query_count = queries.shape[0]
    model_width = queries.shape[1]
    head_size = model_width // head_count
    factor = 1.0 / math.sqrt(head_size)
    query_heads = queries.reshape(query_count, head_count, head_size)
    key_heads = key_rows.reshape(key_rows.shape[0], head_count, head_size)
    value_heads = values.reshape(values.shape[0], head_count, head_size)
    scores = (
        jnp.einsum("qhd,khd->hqk", query_heads, key_heads, preferred_element_type=jnp.float32)
        * factor
    )
    weights = jnp.exp(scores)
    totals = jnp.sum(weights, axis=2).T
    numerator = jnp.einsum(
        "hqk,khd->qhd",
        weights.astype(jnp.bfloat16),
        value_heads,
        preferred_element_type=jnp.float32,
    )
    return (numerator.reshape(query_count, model_width), totals)


def own_terms(every_query, key_rows, values, head_count, row_unit):
    row_total = every_query.shape[0]
    stride = block_size(row_total, row_unit)

    def advance(turn_index, inner_sums):
        offset = turn_index * stride
        query_block = lax.dynamic_slice_in_dim(every_query, offset, stride, 0)
        numerator, totals = partial_terms(query_block, key_rows, values, head_count)
        return (
            lax.dynamic_update_slice_in_dim(inner_sums[0], numerator, offset, 0),
            lax.dynamic_update_slice_in_dim(inner_sums[1], totals, offset, 0),
        )

    starting = (
        jnp.zeros((row_total, key_rows.shape[1]), jnp.float32),
        jnp.zeros((row_total, head_count), jnp.float32),
    )
    return lax.fori_loop(0, row_total // stride, advance, starting)


def attend(queries, own_keys, own_values, head_count):
    query_count = queries.shape[0]
    model_width = queries.shape[1]
    every_query = lax.all_gather(queries, "patch", axis=0, tiled=True)
    numerator, totals = own_terms(every_query, own_keys, own_values, head_count, query_count)
    numerator, totals = (
        lax.psum_scatter(
            numerator.astype(jnp.bfloat16), "patch", scatter_dimension=0, tiled=True
        ).astype(jnp.float32),
        lax.psum_scatter(
            totals.astype(jnp.bfloat16), "patch", scatter_dimension=0, tiled=True
        ).astype(jnp.float32),
    )
    fresh_heads = numerator.reshape(query_count, head_count, -1) / totals[:, :, None]
    return fresh_heads.reshape(query_count, model_width).astype(jnp.bfloat16)


def body(
    tokens,
    projection_weight,
    shift_term,
    scale_term,
    query_gain,
    key_gain,
    stale_keys,
    stale_values,
    stale_output,
    refreshed,
):
    model_width = tokens.shape[1]
    head_count = H
    own_rows = tokens.shape[0]
    own_tiles = own_rows // TILE
    patch_count = lax.axis_size("patch")
    my_index = lax.axis_index("patch")
    share_tiles = own_tiles // 3
    most_tiles = min(own_tiles, share_tiles * patch_count)
    tile_grid = refreshed.reshape(patch_count, own_tiles)
    my_tiles = lax.dynamic_index_in_dim(tile_grid, my_index, 0, keepdims=False)
    picked = jnp.nonzero(my_tiles, size=most_tiles, fill_value=0)[0].astype(jnp.int32)
    token_tiles = tokens.reshape(own_tiles, TILE, model_width)
    chosen = token_tiles[picked].reshape(most_tiles * TILE, model_width)
    hidden = modulate(chosen, shift_term, scale_term)
    projected = jnp.dot(hidden, projection_weight, preferred_element_type=jnp.float32)
    query_new = projected[:, :model_width].astype(jnp.bfloat16)
    key_new = (
        projected[:, model_width : 2 * model_width]
        .astype(jnp.bfloat16)
        .reshape(most_tiles, TILE, model_width)
    )
    value_new = (
        projected[:, 2 * model_width :].astype(jnp.bfloat16).reshape(most_tiles, TILE, model_width)
    )
    position = jnp.maximum(jnp.cumsum(my_tiles) - 1, 0)
    fresh_tile = (my_tiles > 0)[:, None, None]
    keys_all = jnp.where(
        fresh_tile, key_new[position], stale_keys.reshape(own_tiles, TILE, model_width)
    ).reshape(own_rows, model_width)
    values_all = jnp.where(
        fresh_tile, value_new[position], stale_values.reshape(own_tiles, TILE, model_width)
    ).reshape(own_rows, model_width)
    own_keys = head_norm(keys_all, key_gain, head_count)
    queries = head_norm(query_new, query_gain, head_count)
    fresh_rows = attend(queries, own_keys, values_all, head_count)
    fresh_tiles = fresh_rows.reshape(most_tiles, TILE, model_width)
    merged = jnp.where(
        fresh_tile, fresh_tiles[position], stale_output.reshape(own_tiles, TILE, model_width)
    )
    return merged.reshape(own_rows, model_width)


def solution(mesh):
    in_specs = (
        P(("grp", "patch"), None),
        P(),
        P(),
        P(),
        P(),
        P(),
        P(("grp", "patch"), None),
        P(("grp", "patch"), None),
        P(("grp", "patch"), None),
        P("grp"),
    )
    out_specs = P(("grp", "patch"), None)
    return jax.shard_map(body, mesh=mesh, in_specs=in_specs, out_specs=out_specs, check_vma=False)
```

profile of v0, /device:TPU:0, one launch (start us, length us, event | category | flops | bytes accessed | tf_op | source)
XLA Modules:
  0.0 102.9 jit_solution(11285227140400040629)
XLA Ops:
  6.6 0.8 reshape.206
  7.4 0.6 fusion.25
  8.0 0.1 copy.35
  8.1 0.1 fusion.22
  8.3 0.7 scatter_custom_fusion
  9.0 0.1 copy.36
  9.1 0.8 fusion.24
  9.9 0.6 gather_fusion
  10.5 0.2 convert_reduce_fusion
  10.7 0.3 multiply_reduce_fusion.1
  11.0 0.1 div.63
  11.1 0.1 sqrt.28
  11.2 0.3 fusion.17
  11.5 5.8 %convolution_convert_fusion = bf16[256,3456]{1,0:T(8,128)(2,1)S(1)} fusion(bf16[256,1152]{1,0:T(8,128)(2,1)S(1)} %fusion.17, bf16[1152,3456]{1,0:T(8,128)(2,1)} %param.11), kind=kOutput, calls=%fused_computation.10 | convolution fusion | flops 2039316480 | bytes 10321920 | tf_op jit(solution)/shard_map/dot_general | solution.py:121
  17.3 1.2 %copy-done.2 = bf16[256,3456]{1,0:T(8,128)(2,1)} copy-done((bf16[256,3456]{1,0:T(8,128)(2,1)}, bf16[256,3456]{1,0:T(8,128)(2,1)S(1)}, u32[]{:S(2)}) %copy-start.2) | copy-done | bytes 1769496
  18.5 0.1 convert_multiply_fusion
  18.6 0.4 copy.40
  18.9 0.1 reduce_sum.58
  19.2 0.4 copy.41
  19.5 0.2 copy-done.6
  19.7 0.1 mul.54
  19.8 2.1 %fusion.12 = bf16[256,1152]{1,0:T(8,128)(2,1)} fusion(f32[256,1152]{1,0:T(8,128)S(1)} %copy.41, f32[1152]{0:T(1024)S(1)} %mul.54, bf16[256,3456]{1,0:T(8,128)(2,1)} %copy-done.2), kind=kLoop, calls=%fused_computation.19 | loop fusion | flops 1179648 | bytes 2363904 | tf_op jit(solution)/shard_map/convert_element_type | solution.py:23
  22.0 1.3 %fusion.30 = (bf16[256,1152]{1,0:T(8,128)(2,1)S(1)}, bf16[256,1152]{1,0:T(8,128)(2,1)S(1)}) fusion(bf16[256,3456]{1,0:T(8,128)(2,1)} %copy-done.2), kind=kLoop, calls=%fused_computation.60 | loop fusion | bytes 2359296 | tf_op jit(solution)/shard_map/slice | solution.py:129
  23.4 0.1 maximum_reduce_fusion
  23.6 0.1 broadcast_in_dim.29
  23.6 0.7 gather_fusion.2
  24.3 2.6 %fusion.19 = f32[384,1152]{1,0:T(8,128)} fusion(bf16[384,1152]{1,0:T(8,128)(2,1)} %param.16, bf16[24,16,1152]{2,1,0:T(8,128)(2,1)S(1)} %gather_fusion.2, pred[384]{0:T(512)(128)(4,1)S(1)} %broadcast_in_dim.29), kind=kLoop, calls=%fused_computation.31 | loop fusion | flops 884736 | bytes 3539328 | tf_op jit(solution)/shard_map/reshape | solution.py:21
  26.9 2.2 %copy.43 = f32[384,1152]{0,1:T(8,128)S(1)} copy(f32[384,1152]{1,0:T(8,128)} %fusion.19) | data formatting | bytes 3538944 | tf_op jit(solution)/shard_map/reshape | solution.py:21
  29.1 1.6 %gather_fusion.1 = bf16[24,16,1152]{2,1,0:T(8,128)(2,1)} fusion(bf16[16,16,1152]{2,1,0:T(8,128)(2,1)S(1)} %bitcast.50, s32[1024]{0:T(1024)S(1)} %pad_clamp_fusion), kind=kCustom, calls=%fused_computation.1 | custom fusion | bytes 1769568 | tf_op jit(solution)/shard_map/gather | solution.py:137
  30.7 4.7 %gather.20 = bf16[384,16,72]{2,1,0:T(8,128)(2,1)} reshape(bf16[24,16,1152]{2,1,0:T(8,128)(2,1)} %gather_fusion.1) | data formatting | bytes 1769472 | tf_op jit(solution)/shard_map/gather | solution.py:137
  35.4 1.7 %copy.38 = bf16[384,1152]{0,1:T(8,128)(2,1)S(1)} copy(bf16[384,1152]{1,0:T(8,128)(2,1)} %param.17) | data formatting | bytes 1769472 | tf_op args[7]
  37.1 2.0 %copy.39 = bf16[384,16,72]{2,1,0:T(8,128)(2,1)} copy(bf16[384,16,72]{0,2,1:T(8,128)(2,1)S(1)} %bitcast.52) | data formatting | bytes 1769472 | tf_op jit(solution)/shard_map/reshape | solution.py:137
  39.1 0.2 multiply_reduce_fusion
  39.3 1.2 %copy-done.1 = bf16[384,16,72]{2,1,0:T(8,128)(2,1)S(1)} copy-done((bf16[384,16,72]{2,1,0:T(8,128)(2,1)S(1)}, bf16[384,16,72]{2,1,0:T(8,128)(2,1)}, u32[]{:S(2)}) %copy-start.1) | copy-done | bytes 884760
  40.5 3.3 %broadcast_select_fusion = bf16[384,16,72]{2,1,0:T(8,128)(2,1)} fusion(bf16[384,16,72]{2,1,0:T(8,128)(2,1)S(1)} %copy-done.1, bf16[384,16,72]{2,1,0:T(8,128)(2,1)} %copy.39, pred[384]{0:T(512)(128)(4,1)S(1)} %broadcast_in_dim.29), kind=kLoop, calls=%fused_computation.14 | loop fusion | flops 442368 | bytes 2654592 | tf_op jit(solution)/shard_map/jit(_where)/select_n | solution.py:136
  43.8 3.8 %all-gather.2.cloned.1.call-done = bf16[512,1152]{1,0:T(8,128)(2,1)} async-done(((bf16[256,1152]{1,0:T(8,128)(2,1)}), bf16[512,1152]{1,0:T(8,128)(2,1)}) %all-gather.2.cloned.1.call-update) | async-done | bytes 1179664 | tf_op jit(solution)/shard_map/all_gather | solution.py:81
  47.5 2.4 %copy.42 = bf16[512,1152]{0,1:T(8,128)(2,1)} copy(bf16[512,1152]{1,0:T(8,128)(2,1)} %all-gather.2.cloned.1.call-done) | data formatting | bytes 2359296 | tf_op jit(solution)/shard_map/all_gather | solution.py:81
  49.9 8.7 %fusion = (bf16[16,512]{1,0:T(8,128)(2,1)}, f32[16,512,384]{1,2,0:T(8,128)}) fusion(bf16[512,16,72]{0,2,1:T(8,128)(2,1)} %bitcast.53, f32[384,16,72]{0,2,1:T(8,128)S(1)} %bitcast.45, f32[72]{0:T(128)S(1)} %copy-done.7, f32[384,16]{0,1:T(8,128)S(1)} %add_sqrt_fusion), kind=kOutput, calls=%fused_computation.6 | convolution fusion | flops 460595200 | bytes 15573280 | tf_op jit(solution)/shard_map/while/body/eval_jaxpr/qhd,khd->hqk/dot_general | solution.py:44
  58.6 0.2 reduce-scatter.3.cloned.1.call-start
  58.9 8.5 %fusion.6 = bf16[16,72,512]{2,1,0:T(8,128)(2,1)} fusion(f32[16,512,384]{1,2,0:T(8,128)} %get-tuple-element.30, bf16[384,16,72]{2,1,0:T(8,128)(2,1)} %broadcast_select_fusion), kind=kOutput, calls=%fused_computation.15 | convolution fusion | flops 459866112 | bytes 14647296 | tf_op jit(solution)/shard_map/while/body/eval_jaxpr/hqk,khd->qhd/dot_general | solution.py:49
  67.4 1.3 %reduce-scatter.5.cloned.1.call-done = bf16[256,16]{0,1:T(8,128)(2,1)} async-done(((bf16[512,16]{0,1:T(8,128)(2,1)}), bf16[256,16]{0,1:T(8,128)(2,1)}) %reduce-scatter.5.cloned.1.call-update) | async-done | bytes 8208 | tf_op jit(solution)/shard_map/reduce_scatter | solution.py:87
  68.7 0.7 convert_element_type.86
  69.4 23.4 %reduce-scatter.3.cloned.1.call-done = bf16[256,1152]{0,1:T(8,128)(2,1)} async-done(((bf16[512,1152]{0,1:T(8,128)(2,1)}), bf16[256,1152]{0,1:T(8,128)(2,1)}) %reduce-scatter.3.cloned.1.call-update) | async-done | bytes 589840 | tf_op jit(solution)/shard_map/reduce_scatter | solution.py:84
  92.9 1.2 %fusion.13 = bf16[256,1152]{0,1:T(8,128)(2,1)S(1)} fusion(bf16[256,1152]{0,1:T(8,128)(2,1)} %reduce-scatter.3.cloned.1.call-done, f32[256,16]{0,1:T(8,128)S(1)} %convert_element_type.86), kind=kLoop, calls=%fused_computation.21 | loop fusion | flops 884736 | bytes 1196032 | tf_op jit(solution)/shard_map/convert_element_type | solution.py:92
  94.1 0.3 copy.46
  94.4 0.7 gather_fusion.3
  95.0 0.2 copy-done.3
  95.2 1.2 %bitcast_select_fusion = bf16[384,1152]{1,0:T(8,128)(2,1)} fusion(bf16[384,1152]{1,0:T(8,128)(2,1)S(1)} %copy-done.3, bf16[24,16,1152]{2,1,0:T(8,128)(2,1)S(1)} %gather_fusion.3, pred[384]{0:T(512)(128)(4,1)S(1)} %broadcast_in_dim.29), kind=kLoop, calls=%fused_computation.29 | loop fusion | flops 442368 | bytes 2654592 | tf_op jit(solution)/shard_map/jit(_where)/select_n | solution.py:143
  (33 shorter events, 0.5 us)
Async XLA Ops:
  6.5 3.3 %copy-start = (bf16[384,1152]{1,0:T(8,128)(2,1)S(1)}, bf16[384,1152]{1,0:T(8,128)(2,1)}, u32[]{:S(2)}) copy-start(bf16[384,1152]{1,0:T(8,128)(2,1)} %param.10) | copy-start | bytes 2654212
  6.5 4.6 %copy-start.5 = (f32[1152]{0:T(1024)S(1)}, f32[1152]{0:T(1024)}, u32[]{:S(2)}) copy-start(f32[1152]{0:T(1024)} %param.13) | copy-start | bytes 13828
  6.5 4.6 %copy-start.4 = (f32[1152]{0:T(1024)S(1)}, f32[1152]{0:T(1024)}, u32[]{:S(2)}) copy-start(f32[1152]{0:T(1024)} %param.12) | copy-start | bytes 13828
  6.5 41.0 %all-gather.2.cloned.1.call-start = ((), (), s32[]{:S(2)}) async-start(), calls=%async_computation.2 | async-start | bytes 1769472 | tf_op jit(solution)/shard_map/all_gather | solution.py:81
  17.3 1.2 %copy-start.2 = (bf16[256,3456]{1,0:T(8,128)(2,1)}, bf16[256,3456]{1,0:T(8,128)(2,1)S(1)}, u32[]{:S(2)}) copy-start(bf16[256,3456]{1,0:T(8,128)(2,1)S(1)} %convolution_convert_fusion) | copy-start | bytes 5308420
  19.1 0.7 copy-start.6
  21.9 46.8 %reduce-scatter.5.cloned.1.call-start = ((), (), s32[]{:S(2)}) async-start(), calls=%async_computation.4 | async-start | bytes 24576 | tf_op jit(solution)/shard_map/reduce_scatter | solution.py:87
  39.1 1.4 %copy-start.1 = (bf16[384,16,72]{2,1,0:T(8,128)(2,1)S(1)}, bf16[384,16,72]{2,1,0:T(8,128)(2,1)}, u32[]{:S(2)}) copy-start(bf16[384,16,72]{2,1,0:T(8,128)(2,1)} %gather.20) | copy-start | bytes 2654212
  43.8 6.2 %copy-start.7 = (f32[72]{0:T(128)S(1)}, f32[72]{0:T(128)}, u32[]{:S(2)}) copy-start(f32[72]{0:T(128)} %param.15) | copy-start | bytes 868
  58.6 34.2 %reduce-scatter.3.cloned.1.call-start = ((), (), s32[]{:S(2)}) async-start(), calls=%async_computation.3 | async-start | bytes 1769472 | tf_op jit(solution)/shard_map/reduce_scatter | solution.py:84
  94.0 1.2 %copy-start.3 = (bf16[384,1152]{1,0:T(8,128)(2,1)S(1)}, bf16[384,1152]{1,0:T(8,128)(2,1)}, u32[]{:S(2)}) copy-start(bf16[384,1152]{1,0:T(8,128)(2,1)} %param.18) | copy-start | bytes 2654212
Sparse Core Ops, SparseCore 0:
  22.0 25.4 all-gather.1
  58.8 9.9 reduce-scatter.4
  71.0 21.8 reduce-scatter.2
where the time goes:
time: 104 us; the launch traced here: 103 us
  waiting for transfers between devices  28.5 us (27%)
  local copies, waits for them, and re-layouts  23.2 us (22%)
  matrix products  23 us (22%)
  other arithmetic  14.6 us (14%)
  between operations  13.3 us (13%)
    reduce_scatter x1, waiting for transfers between devices, attend(): lax.psum_scatter(numerator.astype(jnp.bfloat16), 'patch', scatter_dimensi...  23.4 us
    dot_general x1, matrix products, partial_terms(): jnp.einsum('qhd,khd->hqk', query_heads, key_heads, preferred_element_type...  8.67 us
    dot_general x1, matrix products, partial_terms(): jnp.einsum('hqk,khd->qhd', weights.astype(jnp.bfloat16), value_heads, pre...  8.54 us
    gather x2, local copies, waits for them, and re-layouts, body(): value_new[position]  6.26 us
    dot_general x1, matrix products, body(): jnp.dot(hidden, projection_weight, preferred_element_type=jnp.float32)  5.78 us
    unnamed x17, local copies, waits for them, and re-layouts  4.56 us
    all_gather x1, waiting for transfers between devices, attend(): every_query = lax.all_gather(queries, 'patch', axis=0, tiled=True)  3.75 us
    select_n x1, other arithmetic, body(): jnp.where(fresh_tile, value_new[position], stale_values.reshape(own_tiles...  3.29 us
  transfers between devices with their start and end apart: 3, of which 3 were waited for; matrix products, arithmetic and copies ran while one was open for 29% of the time, Pallas kernels for 0%

commit v1 on v0

--- a/solution.py
+++ b/solution.py
@@ -78,7 +78,15 @@
 def attend(queries, own_keys, own_values, head_count):
     query_count = queries.shape[0]
     model_width = queries.shape[1]
-    every_query = lax.all_gather(queries, "patch", axis=0, tiled=True)
+    ways, here, step = (lax.axis_size("patch"), lax.axis_index("patch"), queries.shape[0])
+    line, have = (queries, 1)
+    while have < ways:
+        line = jnp.concatenate(
+            [line, lax.ppermute(line, "patch", [(d, (d - have) % ways) for d in range(ways)])],
+            axis=0,
+        )
+        have = 2 * have
+    every_query = jnp.roll(line, here * step, axis=0)
     numerator, totals = own_terms(every_query, own_keys, own_values, head_count, query_count)
     numerator, totals = (
         lax.psum_scatter(

time: 104 us -> 106 us (1.019)
  other arithmetic: 14.6 us -> 20 us
  waiting for transfers between devices: 28.5 us -> 25 us
  starting transfers between devices: 0.27 us -> 3.22 us
  local copies, waits for them, and re-layouts: 23.2 us -> 20.7 us
    all_gather x1 -> x0, waiting for transfers between devices: 3.75 us -> none  [attend(): every_query = lax.all_gather(queries, 'patch', axis=0, tiled=True)]
    concatenate x0 -> x1, other arithmetic: none -> 3.68 us  [attend(): every_query = jnp.roll(line, here * step, axis=0)]
    ppermute x0 -> x1, starting transfers between devices: none -> 3 us  [attend(): lax.ppermute(line, 'patch', [(d, (d - have) % ways) for d in range(ways)])]
    dynamic_slice x0 -> x1, local copies, waits for them, and re-layouts: none -> 2.41 us  [attend(): every_query = jnp.roll(line, here * step, axis=0)]
    all_gather x1 -> x0, local copies, waits for them, and re-layouts: 2.39 us -> none  [attend(): every_query = lax.all_gather(queries, 'patch', axis=0, tiled=True)]
    slice x1, local copies, waits for them, and re-layouts: 1.34 us -> 0.09 us  [body(): projected[:, 2 * model_width:].astype(jnp.bfloat16)]
    unnamed x17, local copies, waits for them, and re-layouts: 4.56 us -> 3.34 us
  transfers between devices with their start and end apart: 3 -> 3, of which waited for: 3 -> 2; matrix products, arithmetic and copies ran while one was open for 29% -> 28% of each run, Pallas kernels for 0% -> 0%
where the time goes in v1:
time: 106 us
  waiting for transfers between devices  25 us (24%)
  matrix products  23 us (22%)
  local copies, waits for them, and re-layouts  20.7 us (20%)
  other arithmetic  20 us (19%)
  between operations  13.6 us (13%)
  starting transfers between devices  3.22 us (3%)
    reduce_scatter x1, waiting for transfers between devices, attend(): lax.psum_scatter(numerator.astype(jnp.bfloat16), 'patch', scatter_dimensi...  23.4 us
    dot_general x1, matrix products, partial_terms(): jnp.einsum('qhd,khd->hqk', query_heads, key_heads, preferred_element_type...  8.67 us
    dot_general x1, matrix products, partial_terms(): jnp.einsum('hqk,khd->qhd', weights.astype(jnp.bfloat16), value_heads, pre...  8.53 us
    gather x2, local copies, waits for them, and re-layouts, body(): value_new[position]  6.21 us
    dot_general x1, matrix products, body(): jnp.dot(hidden, projection_weight, preferred_element_type=jnp.float32)  5.78 us
    concatenate x1, other arithmetic, attend(): every_query = jnp.roll(line, here * step, axis=0)  3.68 us
    select_n x1, other arithmetic, body(): jnp.where(fresh_tile, value_new[position], stale_values.reshape(own_tiles...  3.53 us
    unnamed x17, local copies, waits for them, and re-layouts  3.34 us
  transfers between devices with their start and end apart: 3, of which 2 were waited for; matrix products, arithmetic and copies ran while one was open for 28% of the time, Pallas kernels for 0%

profile of v1, /device:TPU:0, one launch (start us, length us, event | category | flops | bytes accessed | tf_op | source)
XLA Modules:
  0.0 105.5 jit_solution(1337657164635652284)
XLA Ops:
  6.6 0.8 reshape.206
  7.4 0.6 fusion.28
  8.0 0.1 copy.34
  8.1 0.1 fusion.25
  8.3 0.7 scatter_custom_fusion
  9.0 0.1 copy.35
  9.1 0.8 fusion.27
  9.9 0.6 gather_fusion
  10.5 0.2 convert_reduce_fusion
  10.7 0.3 multiply_reduce_fusion.1
  11.0 0.1 div.63
  11.1 0.1 sqrt.28
  11.2 0.3 fusion.20
  11.5 5.8 %convolution_convert_fusion = bf16[256,3456]{1,0:T(8,128)(2,1)S(1)} fusion(bf16[256,1152]{1,0:T(8,128)(2,1)S(1)} %fusion.20, bf16[1152,3456]{1,0:T(8,128)(2,1)} %param.11), kind=kOutput, calls=%fused_computation.10 | convolution fusion | flops 2039316480 | bytes 10321920 | tf_op jit(solution)/shard_map/dot_general | solution.py:129
  17.3 1.2 %copy-done.1 = bf16[256,3456]{1,0:T(8,128)(2,1)} copy-done((bf16[256,3456]{1,0:T(8,128)(2,1)}, bf16[256,3456]{1,0:T(8,128)(2,1)S(1)}, u32[]{:S(2)}) %copy-start.1) | copy-done | bytes 1769496
  18.6 0.4 copy.39
  18.9 0.1 reduce_sum.58
  19.2 0.4 copy.40
  19.5 0.2 copy-done.6
  19.7 0.1 mul.57
  19.8 2.2 %fusion.12 = bf16[256,1152]{1,0:T(8,128)(2,1)} fusion(f32[256,1152]{1,0:T(8,128)S(1)} %copy.40, f32[1152]{0:T(1024)S(1)} %mul.57, bf16[256,3456]{1,0:T(8,128)(2,1)} %copy-done.1), kind=kLoop, calls=%fused_computation.23 | loop fusion | flops 1179648 | bytes 2363904 | tf_op jit(solution)/shard_map/convert_element_type | solution.py:23
  22.0 3.0 %collective-permute-start = (bf16[256,1152]{1,0:T(8,128)(2,1)}, bf16[256,1152]{1,0:T(8,128)(2,1)}, u32[]{:S(2)}, u32[]{:S(2)}) collective-permute-start(bf16[256,1152]{1,0:T(8,128)(2,1)} %fusion.12), channel_id=1, source_target_pairs={{0,1},{1,0},{2,3},{3,2},{4,5},{5,4},{6,7},{7,6},{8,9},{9,8},{10,11... | collective-permute-start | bytes 1769480 | tf_op jit(solution)/shard_map/ppermute | solution.py:85
  25.0 0.1 fusion.33
  25.2 0.1 maximum_reduce_fusion
  25.4 0.1 broadcast_in_dim.29
  25.5 0.7 gather_fusion.2
  26.2 2.6 %fusion.22 = f32[384,1152]{1,0:T(8,128)} fusion(bf16[384,1152]{1,0:T(8,128)(2,1)} %param.16, bf16[24,16,1152]{2,1,0:T(8,128)(2,1)S(1)} %gather_fusion.2, pred[384]{0:T(512)(128)(4,1)S(1)} %broadcast_in_dim.29), kind=kLoop, calls=%fused_computation.38 | loop fusion | flops 884736 | bytes 3539328 | tf_op jit(solution)/shard_map/reshape | solution.py:21
  28.7 2.2 %copy.42 = f32[384,1152]{0,1:T(8,128)S(1)} copy(f32[384,1152]{1,0:T(8,128)} %fusion.22) | data formatting | bytes 3538944 | tf_op jit(solution)/shard_map/reshape | solution.py:21
  30.9 0.8 multiply_reduce_fusion
  31.7 1.6 %gather_fusion.1 = bf16[24,16,1152]{2,1,0:T(8,128)(2,1)} fusion(bf16[16,16,1152]{2,1,0:T(8,128)(2,1)S(1)} %bitcast.50, s32[1024]{0:T(1024)S(1)} %pad_clamp_fusion), kind=kCustom, calls=%fused_computation.1 | custom fusion | bytes 1769568 | tf_op jit(solution)/shard_map/gather | solution.py:145
  33.3 4.6 %gather.20 = bf16[384,16,72]{2,1,0:T(8,128)(2,1)} reshape(bf16[24,16,1152]{2,1,0:T(8,128)(2,1)} %gather_fusion.1) | data formatting | bytes 1769472 | tf_op jit(solution)/shard_map/gather | solution.py:145
  37.9 1.7 %copy.37 = bf16[384,1152]{0,1:T(8,128)(2,1)S(1)} copy(bf16[384,1152]{1,0:T(8,128)(2,1)} %param.17) | data formatting | bytes 1769472 | tf_op args[7]
  39.7 1.9 %copy.38 = bf16[384,16,72]{2,1,0:T(8,128)(2,1)} copy(bf16[384,16,72]{0,2,1:T(8,128)(2,1)S(1)} %bitcast.52) | data formatting | bytes 1769472 | tf_op jit(solution)/shard_map/reshape | solution.py:145
  41.6 0.7 add_sqrt_fusion
  42.4 3.5 %broadcast_select_fusion = bf16[384,16,72]{2,1,0:T(8,128)(2,1)} fusion(bf16[384,16,72]{2,1,0:T(8,128)(2,1)} %gather.20, bf16[384,16,72]{2,1,0:T(8,128)(2,1)} %copy.38, pred[384]{0:T(512)(128)(4,1)S(1)} %broadcast_in_dim.29), kind=kLoop, calls=%fused_computation.18 | loop fusion | flops 442368 | bytes 2654592 | tf_op jit(solution)/shard_map/jit(_where)/select_n | solution.py:144
  45.9 3.7 %fusion.15 = bf16[512,1152]{1,0:T(8,128)(2,1)} fusion(s32[]{:T(128)S(6)} %select_n.97, bf16[256,1152]{1,0:T(8,128)(2,1)} %fusion.12, bf16[256,1152]{1,0:T(8,128)(2,1)} %collective-permute-done), kind=kLoop, calls=%fused_computation.26 | loop fusion | flops 4718592 | bytes 2359300 | tf_op jit(solution)/shard_map/jit(_roll_dynamic)/concatenate | solution.py:89
  49.6 2.4 %copy.41 = bf16[512,1152]{0,1:T(8,128)(2,1)} copy(bf16[512,1152]{1,0:T(8,128)(2,1)} %fusion.15) | data formatting | bytes 2359296 | tf_op jit(solution)/shard_map/jit(_roll_dynamic)/dynamic_slice | solution.py:89
  52.0 8.7 %fusion = (bf16[16,512]{1,0:T(8,128)(2,1)}, f32[16,512,384]{1,2,0:T(8,128)}) fusion(bf16[512,16,72]{0,2,1:T(8,128)(2,1)} %bitcast.53, f32[384,16,72]{0,2,1:T(8,128)S(1)} %bitcast.45, f32[72]{0:T(128)S(1)} %copy-done.7, f32[384,16]{0,1:T(8,128)S(1)} %add_sqrt_fusion), kind=kOutput, calls=%fused_computation.6 | convolution fusion | flops 460595200 | bytes 15573280 | tf_op jit(solution)/shard_map/while/body/eval_jaxpr/qhd,khd->hqk/dot_general | solution.py:44
  60.7 0.2 reduce-scatter.3.cloned.1.call-start
  60.9 8.5 %fusion.6 = bf16[16,72,512]{2,1,0:T(8,128)(2,1)} fusion(f32[16,512,384]{1,2,0:T(8,128)} %get-tuple-element.30, bf16[384,16,72]{2,1,0:T(8,128)(2,1)} %broadcast_select_fusion), kind=kOutput, calls=%fused_computation.19 | convolution fusion | flops 459866112 | bytes 14647296 | tf_op jit(solution)/shard_map/while/body/eval_jaxpr/hqk,khd->qhd/dot_general | solution.py:49
  69.5 1.6 %reduce-scatter.5.cloned.1.call-done = bf16[256,16]{0,1:T(8,128)(2,1)} async-done(((bf16[512,16]{0,1:T(8,128)(2,1)}), bf16[256,16]{0,1:T(8,128)(2,1)}) %reduce-scatter.5.cloned.1.call-update) | async-done | bytes 8208 | tf_op jit(solution)/shard_map/reduce_scatter | solution.py:95
  71.1 0.7 convert_element_type.86
  71.8 23.4 %reduce-scatter.3.cloned.1.call-done = bf16[256,1152]{0,1:T(8,128)(2,1)} async-done(((bf16[512,1152]{0,1:T(8,128)(2,1)}), bf16[256,1152]{0,1:T(8,128)(2,1)}) %reduce-scatter.3.cloned.1.call-update) | async-done | bytes 589840 | tf_op jit(solution)/shard_map/reduce_scatter | solution.py:92
  95.2 1.2 %fusion.16 = bf16[256,1152]{0,1:T(8,128)(2,1)S(1)} fusion(bf16[256,1152]{0,1:T(8,128)(2,1)} %reduce-scatter.3.cloned.1.call-done, f32[256,16]{0,1:T(8,128)S(1)} %convert_element_type.86), kind=kLoop, calls=%fused_computation.28 | loop fusion | flops 884736 | bytes 1196032 | tf_op jit(solution)/shard_map/convert_element_type | solution.py:100
  96.4 0.3 copy.45
  96.7 0.7 gather_fusion.3
  97.4 0.2 copy-done.3
  97.5 1.2 %bitcast_select_fusion = bf16[384,1152]{1,0:T(8,128)(2,1)} fusion(bf16[384,1152]{1,0:T(8,128)(2,1)S(1)} %copy-done.3, bf16[24,16,1152]{2,1,0:T(8,128)(2,1)S(1)} %gather_fusion.3, pred[384]{0:T(512)(128)(4,1)S(1)} %broadcast_in_dim.29), kind=kLoop, calls=%fused_computation.36 | loop fusion | flops 442368 | bytes 2654592 | tf_op jit(solution)/shard_map/jit(_where)/select_n | solution.py:151
  (33 shorter events, 0.5 us)
Async XLA Ops:
  6.5 3.3 %copy-start = (bf16[384,1152]{1,0:T(8,128)(2,1)S(1)}, bf16[384,1152]{1,0:T(8,128)(2,1)}, u32[]{:S(2)}) copy-start(bf16[384,1152]{1,0:T(8,128)(2,1)} %param.10) | copy-start | bytes 2654212
  6.5 4.6 %copy-start.5 = (f32[1152]{0:T(1024)S(1)}, f32[1152]{0:T(1024)}, u32[]{:S(2)}) copy-start(f32[1152]{0:T(1024)} %param.13) | copy-start | bytes 13828
  6.5 4.6 %copy-start.4 = (f32[1152]{0:T(1024)S(1)}, f32[1152]{0:T(1024)}, u32[]{:S(2)}) copy-start(f32[1152]{0:T(1024)} %param.12) | copy-start | bytes 13828
  6.5 64.5 %reduce-scatter.5.cloned.1.call-start = ((), (), s32[]{:S(2)}) async-start(), calls=%async_computation.3 | async-start | bytes 24576 | tf_op jit(solution)/shard_map/reduce_scatter | solution.py:95
  17.3 1.2 %copy-start.1 = (bf16[256,3456]{1,0:T(8,128)(2,1)}, bf16[256,3456]{1,0:T(8,128)(2,1)S(1)}, u32[]{:S(2)}) copy-start(bf16[256,3456]{1,0:T(8,128)(2,1)S(1)} %convolution_convert_fusion) | copy-start | bytes 5308420
  19.1 0.7 copy-start.6
  19.8 5.2 %copy-start.2 = (bf16[256,3456]{1,0:T(8,128)(2,1)S(1)}, bf16[256,3456]{1,0:T(8,128)(2,1)}, u32[]{:S(2)}) copy-start(bf16[256,3456]{1,0:T(8,128)(2,1)} %copy-done.1) | copy-start | bytes 5308420
  22.0 23.9 %collective-permute-start = (bf16[256,1152]{1,0:T(8,128)(2,1)}, bf16[256,1152]{1,0:T(8,128)(2,1)}, u32[]{:S(2)}, u32[]{:S(2)}) collective-permute-start(bf16[256,1152]{1,0:T(8,128)(2,1)} %fusion.12), channel_id=1, source_target_pairs={{0,1},{1,0},{2,3},{3,2},{4,5},{5,4},{6,7},{7,6},{8,9},{9,8},{10,11... | collective-permute-start | bytes 1769480 | tf_op jit(solution)/shard_map/ppermute | solution.py:85
  49.6 2.4 %copy-start.7 = (f32[72]{0:T(128)S(1)}, f32[72]{0:T(128)}, u32[]{:S(2)}) copy-start(f32[72]{0:T(128)} %param.15) | copy-start | bytes 868
  60.7 34.5 %reduce-scatter.3.cloned.1.call-start = ((), (), s32[]{:S(2)}) async-start(), calls=%async_computation.2 | async-start | bytes 1769472 | tf_op jit(solution)/shard_map/reduce_scatter | solution.py:92
  96.4 1.2 %copy-start.3 = (bf16[384,1152]{1,0:T(8,128)(2,1)S(1)}, bf16[384,1152]{1,0:T(8,128)(2,1)}, u32[]{:S(2)}) copy-start(bf16[384,1152]{1,0:T(8,128)(2,1)} %param.18) | copy-start | bytes 2654212
Sparse Core Ops, SparseCore 0:
  60.8 10.2 reduce-scatter.4
  73.3 21.8 reduce-scatter.2
